TPU v7x, 256 devices: a whole 4x4x8 slice. The times are simulated.
256 devices in a mesh: dp: 4 (over y), tensor: 16 (over z, core), owner: 4 (over x).
Axes of the slice: x: 4, y: 4, z: 8, core: 2. Of those that a mesh axis runs over, the one named last changes fastest.
Arguments:
- queries: bfloat16 [512, 8192], P(('dp', 'tensor'), 'owner'), may hold values from -360 to 360
- cached_key_rows: bfloat16 [512, 512, 8, 128], P(('dp', 'tensor'), None, 'owner'), may hold values from -6 to 6
- cached_value_rows: bfloat16 [512, 512, 8, 128], P(('dp', 'tensor'), None, 'owner'), may hold values from -6 to 6
- newest_key: bfloat16 [512, 8, 128], P(('dp', 'tensor'), 'owner'), may hold values from -6 to 6
- newest_value: bfloat16 [512, 8, 128], P(('dp', 'tensor'), 'owner'), may hold values from -6 to 6
- output_weight: bfloat16 [8, 1024, 8192], P('owner', 'tensor'), may hold values from -0.75 to 0.75
- adapter_down_weight: bfloat16 [128, 8, 1024, 64], P('owner', None, 'tensor'), may hold values from -0.5 to 0.5
- adapter_up_weight: bfloat16 [128, 64, 8192], P('owner', None, 'tensor'), may hold values from -0.75 to 0.75
- adapter_store_row: int32 [128], replicated, may hold values from 0 to 127, each once
- adapters_by_group: int32 [4, 16], P('dp'), may hold values from 0 to 127, as said below
- adapter_per_row: int32 [512], P('dp'), may hold values from 0 to 127, as said below
Outputs:
- output: bfloat16 [512, 8192], P('dp', ('tensor', 'owner'))
Inputs may be any that keep to these rules, and one draw needn't show every extreme that they name: `adapter_per_row`: the rows g * 128 to (g + 1) * 128 - 1 form dp group g; each row's adapter is one of its group's listed adapters, and each listed one is used by some row of the group. `adapters_by_group`: the 16 adapters of a group are distinct.
All inputs are finite; a program needn't handle non-finite values.
Results may differ from a plain program's by a relative error of at most 0.015.
Values may be sent and summed in bfloat16 or wider, within the bound.
No kernel may reach another device: no remote copies, remote signals or barrier semaphores. Data moves between devices by JAX's collectives and lax.ppermute only.
A program may use at most 128 MiB of HBM per device.

v0:
```python
import jax
import jax.numpy as jnp
from jax import lax
from jax.sharding import PartitionSpec as P

ADAPTER_SCALE = 2.0


def shards(
    queries,
    cached_key_rows,
    cached_value_rows,
    newest_key,
    newest_value,
    output_weight,
    adapter_down_weight,
    adapter_up_weight,
    adapter_store_row,
    adapters_by_group,
    adapter_per_row,
):
    owner_index = lax.axis_index("owner")
    row_count = queries.shape[0]
    local_heads = newest_key.shape[1]
    head_width = newest_key.shape[2]
    group_width = queries.shape[1] // local_heads
    query_heads = queries.reshape(row_count, local_heads, group_width // head_width, head_width)
    inverse_root = head_width ** (-0.5)
    scores = (
        jnp.einsum(
            "rkgh,rckh->rkgc", query_heads, cached_key_rows, preferred_element_type=jnp.float32
        )
        * inverse_root
    )
    fresh_score = (
        jnp.einsum("rkgh,rkh->rkg", query_heads, newest_key, preferred_element_type=jnp.float32)
        * inverse_root
    )
    overall = jnp.maximum(jnp.max(scores, axis=-1), fresh_score)
    weights_exp = jnp.exp(scores - overall[..., None])
    fresh_weight = jnp.exp(fresh_score - overall)
    denominator = jnp.sum(weights_exp, axis=-1) + fresh_weight
    mixed = jnp.einsum(
        "rkgc,rckh->rkgh", weights_exp, cached_value_rows, preferred_element_type=jnp.float32
    )
    mixed = mixed + fresh_weight[..., None] * newest_value.astype(jnp.float32)[:, :, None, :]
    mixed = (
        (mixed / denominator[..., None])
        .astype(jnp.bfloat16)
        .reshape(row_count, local_heads, group_width)
    )
    attention = lax.all_to_all(mixed, "tensor", split_axis=2, concat_axis=0, tiled=True)
    slot_ids = adapters_by_group[0]
    adapter_total = adapter_store_row.shape[0]
    matches = slot_ids[:, None] == jnp.arange(adapter_total, dtype=jnp.int32)[None, :]
    slot_home = jnp.sum(jnp.where(matches, adapter_store_row[None, :], 0), axis=1)
    store_count = adapter_down_weight.shape[0]
    slot_match = (adapter_per_row[:, None] == slot_ids[None, :]).astype(jnp.float32)
    position = slot_home - owner_index * store_count
    is_present = (position >= 0) & (position < store_count)
    clamped_index = jnp.clip(position, 0, store_count - 1)
    down_projected = jnp.where(
        is_present[:, None, None, None], adapter_down_weight[clamped_index], 0
    )
    up_projected = jnp.where(is_present[:, None, None], adapter_up_weight[clamped_index], 0)
    down_total, up_total = (
        lax.psum_scatter(down_projected, "owner", scatter_dimension=1, tiled=True).astype(
            jnp.float32
        ),
        lax.psum_scatter(up_projected, "owner", scatter_dimension=2, tiled=True).astype(
            jnp.float32
        ),
    )
    slot_down = down_total.astype(jnp.bfloat16)
    slot_up = up_total.astype(jnp.bfloat16)
    rank_slots = jnp.einsum(
        "rkf,skfn->rsn", attention, slot_down, preferred_element_type=jnp.float32
    )
    rank_part = jnp.sum(slot_match[:, :, None] * rank_slots, axis=1)
    rank_code = lax.psum(rank_part, ("tensor", "owner")).astype(jnp.bfloat16)
    update_slots = jnp.einsum("rn,snc->rsc", rank_code, slot_up, preferred_element_type=jnp.float32)
    adapter_delta = jnp.sum(slot_match[:, :, None] * update_slots, axis=1)
    partial_sum = jnp.einsum(
        "rkf,kfd->rd", attention, output_weight, preferred_element_type=jnp.float32
    )
    base_output = lax.psum_scatter(
        partial_sum, ("tensor", "owner"), scatter_dimension=1, tiled=True
    )
    return (base_output + ADAPTER_SCALE * adapter_delta).astype(jnp.bfloat16)


def solution(mesh):
    return jax.shard_map(
        shards,
        mesh=mesh,
        in_specs=(
            P(("dp", "tensor"), "owner"),
            P(("dp", "tensor"), None, "owner", None),
            P(("dp", "tensor"), None, "owner", None),
            P(("dp", "tensor"), "owner", None),
            P(("dp", "tensor"), "owner", None),
            P("owner", "tensor", None),
            P("owner", None, "tensor", None),
            P("owner", None, "tensor"),
            P(),
            P("dp", None),
            P("dp"),
        ),
        out_specs=P("dp", ("tensor", "owner")),
        check_vma=False,
    )
```

profile of v0, /device:TPU:8, one launch (start us, length us, event | category | flops | bytes accessed | tf_op | source)
XLA Modules:
  0.0 342.8 jit_solution(8786427746575031881)
XLA Ops:
  6.5 0.0 copy-start
  6.5 0.0 all-reduce.3.cloned.1.call-start
  6.5 1.0 select_reduce_fusion
  7.6 4.3 %gather_fusion = bf16[16,8,64,64]{3,2,1,0:T(8,128)(2,1)} fusion(bf16[32,8,64,64]{3,2,1,0:T(8,128)(2,1)} %param.17, s32[1024]{0:T(1024)S(1)} %pad_clamp_fusion), kind=kCustom, calls=%fused_computation | custom fusion | bytes 2097216 | tf_op jit(solution)/shard_map/gather | solution.py:63
  11.9 3.1 broadcast_select_fusion
  15.1 0.0 all-reduce.3.cloned.1.call-update
  15.1 0.0 reduce-scatter.8.cloned.1.call-start
  15.1 3.2 gather_fusion.1
  18.3 1.4 broadcast_select_fusion.1
  19.7 2.9 copy.60
  22.6 0.0 copy-start.2
  22.6 0.0 copy-start.1
  22.6 0.0 copy-start.6
  22.6 4.2 %reshape.104 = bf16[512,1024]{1,0:T(8,128)(2,1)} reshape(bf16[512,16,64]{2,1,0:T(8,128)(2,1)} %bitcast.44) | data formatting | bytes 2097152
  26.8 0.0 reduce-scatter.8.cloned.1.call-update
  26.8 0.0 reduce-scatter.6.cloned.1.call-start
  26.9 0.0 copy-done.2
  26.9 0.0 copy-start.5
  26.9 0.0 copy-done.1
  26.9 0.0 copy-done.6
  26.9 0.1 fusion.25
  27.0 2.4 fusion.34
  29.5 0.2 fusion.21
  29.7 0.0 copy-done.5
  29.8 0.5 fusion.16
  30.2 0.3 copy.54
  30.5 0.5 reshape.107
  31.1 16.3 %all_to_all.18 = bf16[16,2,512]{2,1,0:T(2,128)(2,1)S(1)} all-to-all(bf16[16,2,512]{2,1,0:T(2,128)(2,1)S(1)} %reshape.107), channel_id=1, replica_groups=mesh['dp'=4,'tensor'=16,'owner'=4] {'tensor'}, dimensions={0} | all-to-all | bytes 65536 | tf_op jit(solution)/shard_map/all_to_all | solution.py:52
  47.3 0.6 reshape.108
  48.0 0.4 copy.56
  48.4 0.0 copy-done
  48.4 2.7 convolution_bitcast_fusion
  51.0 0.0 copy-start.7
  51.0 0.0 copy-start.3
  51.0 0.0 copy-start.4
  51.1 0.0 reduce-scatter.6.cloned.1.call-update
  51.1 0.6 copy-done.7
  51.7 0.6 dynamic-slice
  53.0 0.0 copy-done.3
  53.0 0.0 copy-done.4
  53.0 0.1 compare_convert_fusion
  53.1 28.9 %all-reduce.3.cloned.1.call-done = bf16[16,8,64,64]{3,2,1,0:T(8,128)(2,1)} async-done(((bf16[16,8,64,64]{3,2,1,0:T(8,128)(2,1)}), bf16[16,8,64,64]{3,2,1,0:T(8,128)(2,1)}) %all-reduce.3.cloned.1.call-update) | async-done | bytes 1048592
  81.9 1.4 fusion.6
  83.3 249.7 %psum.7 = bf16[128,64]{0,1:T(8,128)(2,1)S(1)} all-reduce(f32[128,64]{0,1:T(8,128)S(1)} %fusion.6), channel_id=1, replica_groups=mesh['dp'=4,'tensor'=16,'owner'=4] {'tensor','owner'}, use_global_device_ids=true, to_apply=%region_6.7 | all-reduce | flops 8192 | bytes 49152 | tf_op jit(solution)/shard_map/psum | solution.py:80
  333.0 1.3 reshape.105
  334.4 0.4 fusion.4
  334.8 0.0 reduce-scatter.6.cloned.1.call-done
  334.8 1.5 add_convert_fusion
  (7 shorter events, 0.1 us)
Async XLA Ops:
  6.5 41.8 %copy-start = (bf16[2,64,8192]{2,1,0:T(8,128)(2,1)S(1)}, bf16[2,64,8192]{2,1,0:T(8,128)(2,1)}, u32[]{:S(2)}) copy-start(bf16[2,64,8192]{2,1,0:T(8,128)(2,1)} %param.16) | copy-start | bytes 6291460
  6.5 75.4 %all-reduce.3.cloned.1.call-start = ((), (), s32[]{:S(2)}) async-start(), calls=%async_computation.5 | async-start | bytes 4194304
  15.1 317.9 %reduce-scatter.8.cloned.1.call-start = ((), (), s32[]{:S(2)}) async-start(), calls=%async_computation.4 | async-start | bytes 1310720
  22.6 4.2 %copy-start.2 = (bf16[8,2,128]{2,1,0:T(2,128)(2,1)S(1)}, bf16[8,2,128]{2,1,0:T(2,128)(2,1)}, u32[]{:S(2)}) copy-start(bf16[8,2,128]{2,1,0:T(2,128)(2,1)} %param.15) | copy-start | bytes 12292
  22.6 4.3 %copy-start.1 = (bf16[8,2048]{1,0:T(8,128)(2,1)S(1)}, bf16[8,2048]{1,0:T(8,128)(2,1)}, u32[]{:S(2)}) copy-start(bf16[8,2048]{1,0:T(8,128)(2,1)} %param.11) | copy-start | bytes 98308
  22.6 4.3 %copy-start.6 = (bf16[8,2,128]{2,1,0:T(2,128)(2,1)S(1)}, bf16[8,2,128]{2,1,0:T(2,128)(2,1)}, u32[]{:S(2)}) copy-start(bf16[8,2,128]{2,1,0:T(2,128)(2,1)} %param.14) | copy-start | bytes 12292
  26.8 308.0 %reduce-scatter.6.cloned.1.call-start = ((), (), s32[]{:S(2)}) async-start(), calls=%async_computation.3 | async-start | bytes 4259840 | tf_op jit(solution)/shard_map/reduce_scatter | solution.py:86
  26.9 2.9 copy-start.5
  51.0 0.7 copy-start.7
  51.0 1.9 copy-start.3
  51.0 1.9 copy-start.4
Sparse Core Ops, SparseCore 0:
  15.2 66.6 all-reduce.2
  84.6 25.9 reduce-scatter.7
  114.8 143.6 reduce-scatter.5
where the time goes:
time: 343 us
  blocking collectives  266 us (78%)
  waiting for transfers between devices  28.9 us (8%)
  local copies, waits for them, and re-layouts  19 us (6%)
  between operations  13.9 us (4%)
  matrix products  7.54 us (2%)
  other arithmetic  7.3 us (2%)
    psum x1, blocking collectives, shards(): rank_code = lax.psum(rank_part, ('tensor', 'owner')).astype(jnp.bfloat16)  250 us
    unnamed x5, waiting for transfers between devices  28.9 us
    all_to_all x1, blocking collectives, shards(): lax.all_to_all(mixed, 'tensor', split_axis=2, concat_axis=0, tiled=True)  16.3 us
    unnamed x22, local copies, waits for them, and re-layouts  10.8 us
  transfers between devices with their start and end apart: 3, of which 1 were waited for; matrix products, arithmetic and copies ran while one was open for 7% of the time, Pallas kernels for 0%

commit v1 on v0

--- a/solution.py
+++ b/solution.py
@@ -77,7 +77,7 @@
         "rkf,skfn->rsn", attention, slot_down, preferred_element_type=jnp.float32
     )
     rank_part = jnp.sum(slot_match[:, :, None] * rank_slots, axis=1)
-    rank_code = lax.psum(rank_part, ("tensor", "owner")).astype(jnp.bfloat16)
+    rank_code = lax.psum(lax.psum(rank_part, "tensor"), "owner").astype(jnp.bfloat16)
     update_slots = jnp.einsum("rn,snc->rsc", rank_code, slot_up, preferred_element_type=jnp.float32)
     adapter_delta = jnp.sum(slot_match[:, :, None] * update_slots, axis=1)
     partial_sum = jnp.einsum(

time: 343 us -> 267 us (0.78)
  blocking collectives: 266 us -> 80.6 us
  waiting for transfers between devices: 28.9 us -> 138 us
    psum x1 -> x2, blocking collectives: 250 us -> 64.3 us  [the longest x1 48.7 us: shards(): lax.psum(rank_part, 'tensor')]
    reduce_scatter x1, waiting for transfers between devices: 0.02 us -> 109 us  [shards(): lax.psum_scatter(partial_sum, ('tensor', 'owner'), scatter_dimension=1, t...]
  transfers between devices with their start and end apart: 3 -> 3, of which waited for: 1 -> 2; matrix products, arithmetic and copies ran while one was open for 7% -> 9% of each run, Pallas kernels for 0% -> 0%
where the time goes in v1:
time: 267 us; the launch traced here: 266 us
  waiting for transfers between devices  138 us (52%)
  blocking collectives  80.6 us (30%)
  local copies, waits for them, and re-layouts  19 us (7%)
  between operations  13.9 us (5%)
  matrix products  7.53 us (3%)
  other arithmetic  7.3 us (3%)
    reduce_scatter x1, waiting for transfers between devices, shards(): lax.psum_scatter(partial_sum, ('tensor', 'owner'), scatter_dimension=1, t...  109 us
    psum x1, blocking collectives, shards(): lax.psum(rank_part, 'tensor')  48.7 us
    unnamed x5, waiting for transfers between devices  28.9 us
    all_to_all x1, blocking collectives, shards(): lax.all_to_all(mixed, 'tensor', split_axis=2, concat_axis=0, tiled=True)  16.3 us
    psum x1, blocking collectives, shards(): lax.psum(lax.psum(rank_part, 'tensor'), 'owner').astype(jnp.bfloat16)  15.6 us
    unnamed x22, local copies, waits for them, and re-layouts  10.8 us
  transfers between devices with their start and end apart: 3, of which 2 were waited for; matrix products, arithmetic and copies ran while one was open for 9% of the time, Pallas kernels for 0%

profile of v1, /device:TPU:8, one launch (start us, length us, event | category | flops | bytes accessed | tf_op | source)
XLA Modules:
  0.0 266.4 jit_solution(18204282053482980457)
XLA Ops:
  6.5 0.0 copy-start
  6.5 0.0 all-reduce.3.cloned.1.call-start
  6.5 1.0 select_reduce_fusion
  7.6 4.3 %gather_fusion = bf16[16,8,64,64]{3,2,1,0:T(8,128)(2,1)} fusion(bf16[32,8,64,64]{3,2,1,0:T(8,128)(2,1)} %param.17, s32[1024]{0:T(1024)S(1)} %pad_clamp_fusion), kind=kCustom, calls=%fused_computation | custom fusion | bytes 2097216 | tf_op jit(solution)/shard_map/gather | solution.py:63
  11.9 3.1 %broadcast_select_fusion = bf16[16,8,64,64]{3,2,1,0:T(8,128)(2,1)} fusion(bf16[16,8,64,64]{3,2,1,0:T(8,128)(2,1)} %gather_fusion, pred[16]{0:T(512)(128)(4,1)S(1)} %compare_and_fusion), kind=kLoop, calls=%fused_computation.7 | loop fusion | flops 524288 | bytes 2097168 | tf_op jit(solution)/shard_map/jit(_where)/select_n | solution.py:62
  15.1 0.0 all-reduce.3.cloned.1.call-update
  15.1 0.0 reduce-scatter.8.cloned.1.call-start
  15.1 3.2 %gather_fusion.1 = bf16[16,64,512]{2,1,0:T(8,128)(2,1)} fusion(bf16[32,64,512]{2,1,0:T(8,128)(2,1)} %param.18, s32[1024]{0:T(1024)S(1)} %pad_clamp_fusion), kind=kCustom, calls=%fused_computation.1 | custom fusion | bytes 2097216 | tf_op jit(solution)/shard_map/gather | solution.py:65
  18.3 1.4 broadcast_select_fusion.1
  19.7 2.9 %copy.60 = bf16[16,64,512]{1,0,2:T(8,128)(2,1)} copy(bf16[16,64,512]{2,1,0:T(8,128)(2,1)S(1)} %broadcast_select_fusion.1) | data formatting | bytes 2097152
  22.6 0.0 copy-start.2
  22.6 0.0 copy-start.1
  22.6 0.0 copy-start.6
  22.6 4.2 %reshape.104 = bf16[512,1024]{1,0:T(8,128)(2,1)} reshape(bf16[512,16,64]{2,1,0:T(8,128)(2,1)} %bitcast.44) | data formatting | bytes 2097152
  26.8 0.0 reduce-scatter.8.cloned.1.call-update
  26.8 0.0 reduce-scatter.6.cloned.1.call-start
  26.9 0.0 copy-done.2
  26.9 0.0 copy-start.5
  26.9 0.0 copy-done.1
  26.9 0.0 copy-done.6
  26.9 0.1 fusion.25
  27.0 2.4 fusion.34
  29.5 0.2 fusion.21
  29.7 0.0 copy-done.5
  29.8 0.5 fusion.16
  30.2 0.3 copy.54
  30.5 0.5 reshape.107
  31.1 16.3 %all_to_all.18 = bf16[16,2,512]{2,1,0:T(2,128)(2,1)S(1)} all-to-all(bf16[16,2,512]{2,1,0:T(2,128)(2,1)S(1)} %reshape.107), channel_id=1, replica_groups=mesh['dp'=4,'tensor'=16,'owner'=4] {'tensor'}, dimensions={0} | all-to-all | bytes 65536 | tf_op jit(solution)/shard_map/all_to_all | solution.py:52
  47.3 0.6 reshape.108
  48.0 0.4 copy.56
  48.4 0.0 copy-done
  48.4 2.7 %convolution_bitcast_fusion = f32[128,8192]{1,0:T(8,128)} fusion(bf16[2,64,8192]{2,1,0:T(8,128)(2,1)S(1)} %copy-done, bf16[8,2,16,64]{3,0,2,1:T(8,128)(2,1)S(1)} %copy.56), kind=kOutput, calls=%fused_computation.2 | convolution fusion | flops 268435456 | bytes 6324224 | tf_op jit(solution)/shard_map/rkf,kfd->rd/dot_general | solution.py:83
  51.0 0.0 copy-start.7
  51.1 0.0 reduce-scatter.6.cloned.1.call-update
  51.1 0.6 copy-done.7
  51.7 0.6 dynamic-slice
  53.0 0.0 copy-done.3
  53.0 0.0 copy-done.4
  53.0 0.1 compare_convert_fusion
  53.1 28.9 %all-reduce.3.cloned.1.call-done = bf16[16,8,64,64]{3,2,1,0:T(8,128)(2,1)} async-done(((bf16[16,8,64,64]{3,2,1,0:T(8,128)(2,1)}), bf16[16,8,64,64]{3,2,1,0:T(8,128)(2,1)}) %all-reduce.3.cloned.1.call-update) | async-done | bytes 1048592
  81.9 1.4 fusion.6
  83.3 48.7 %psum.14 = f32[128,64]{0,1:T(8,128)S(1)} all-reduce(f32[128,64]{0,1:T(8,128)S(1)} %fusion.6), channel_id=1, replica_groups=mesh['dp'=4,'tensor'=16,'owner'=4] {'tensor'}, use_global_device_ids=true, to_apply=%region_6.7 | all-reduce | flops 8192 | bytes 65536 | tf_op jit(solution)/shard_map/psum | solution.py:80
  132.0 15.6 %psum.15 = bf16[128,64]{0,1:T(8,128)(2,1)S(1)} all-reduce(f32[128,64]{0,1:T(8,128)S(1)} %psum.14), channel_id=1, replica_groups=mesh['dp'=4,'tensor'=16,'owner'=4] {'owner'}, use_global_device_ids=true, to_apply=%region_7.8 | all-reduce | flops 8192 | bytes 49152 | tf_op jit(solution)/shard_map/psum | solution.py:80
  147.6 0.0 reduce-scatter.8.cloned.1.call-done
  147.6 1.3 reshape.105
  149.0 0.4 fusion.4
  149.4 109.0 %reduce-scatter.6.cloned.1.call-done = f32[128,128]{1,0:T(8,128)} async-done(((f32[128,8192]{1,0:T(8,128)}), f32[128,128]{1,0:T(8,128)}) %reduce-scatter.6.cloned.1.call-update) | async-done | bytes 65552 | tf_op jit(solution)/shard_map/reduce_scatter | solution.py:86
  258.4 1.5 add_convert_fusion
  (8 shorter events, 0.1 us)
Async XLA Ops:
  6.5 41.8 %copy-start = (bf16[2,64,8192]{2,1,0:T(8,128)(2,1)S(1)}, bf16[2,64,8192]{2,1,0:T(8,128)(2,1)}, u32[]{:S(2)}) copy-start(bf16[2,64,8192]{2,1,0:T(8,128)(2,1)} %param.16) | copy-start | bytes 6291460
  6.5 75.4 %all-reduce.3.cloned.1.call-start = ((), (), s32[]{:S(2)}) async-start(), calls=%async_computation.5 | async-start | bytes 4194304
  15.1 132.5 %reduce-scatter.8.cloned.1.call-start = ((), (), s32[]{:S(2)}) async-start(), calls=%async_computation.4 | async-start | bytes 1310720
  22.6 4.2 %copy-start.2 = (bf16[8,2,128]{2,1,0:T(2,128)(2,1)S(1)}, bf16[8,2,128]{2,1,0:T(2,128)(2,1)}, u32[]{:S(2)}) copy-start(bf16[8,2,128]{2,1,0:T(2,128)(2,1)} %param.15) | copy-start | bytes 12292
  22.6 4.3 %copy-start.1 = (bf16[8,2048]{1,0:T(8,128)(2,1)S(1)}, bf16[8,2048]{1,0:T(8,128)(2,1)}, u32[]{:S(2)}) copy-start(bf16[8,2048]{1,0:T(8,128)(2,1)} %param.11) | copy-start | bytes 98308
  22.6 4.3 %copy-start.6 = (bf16[8,2,128]{2,1,0:T(2,128)(2,1)S(1)}, bf16[8,2,128]{2,1,0:T(2,128)(2,1)}, u32[]{:S(2)}) copy-start(bf16[8,2,128]{2,1,0:T(2,128)(2,1)} %param.14) | copy-start | bytes 12292
  26.8 231.6 %reduce-scatter.6.cloned.1.call-start = ((), (), s32[]{:S(2)}) async-start(), calls=%async_computation.3 | async-start | bytes 4259840 | tf_op jit(solution)/shard_map/reduce_scatter | solution.py:86
  26.9 2.9 %copy-start.5 = (bf16[8,512,2,128]{3,2,1,0:T(2,128)(2,1)S(1)}, bf16[8,512,2,128]{3,2,1,0:T(2,128)(2,1)}, u32[]{:S(2)}) copy-start(bf16[8,512,2,128]{3,2,1,0:T(2,128)(2,1)} %param.13) | copy-start | bytes 6291460
  51.0 0.7 copy-start.7
  51.0 1.9 copy-start.3
  51.0 1.9 copy-start.4
Sparse Core Ops, SparseCore 0:
  15.2 66.6 all-reduce.2
  84.6 25.8 reduce-scatter.7
  114.7 143.6 reduce-scatter.5
